TPU v7x, 256 devices: a whole 4x4x8 slice. The times are simulated.
256 devices in a mesh: req: 16 (over z_hi, y, core), tp: 16 (over z_lo, x).
Axes of the slice: x: 4, y: 4, z: 8 (z_hi: 2, z_lo: 4; z = z_hi * 4 + z_lo), core: 2. Of those that a mesh axis runs over, the one named last changes fastest.
Arguments:
- queries: bfloat16 [64, 32, 4096], P('req'), may hold values from -128 to 128
- cache_keys: bfloat16 [64, 4096, 512], P('req', 'tp'), may hold values from -4 to 4
- cache_values: bfloat16 [64, 4096, 512], P('req', 'tp'), may hold values from -5 to 5
- tree_keys: bfloat16 [64, 32, 512], P('req', 'tp'), may hold values from -5 to 5
- tree_values: bfloat16 [64, 32, 512], P('req', 'tp'), may hold values from -5 to 5
- parents: int32 [64, 32], P('req'), may hold values from -1 to 30, as said below
- lengths: int32 [64], P('req'), may hold values from 2 to 4096
- accepted_leaf: int32 [64], P('req'), may hold values from 0 to 31
- residual: bfloat16 [64, 32, 8192], P('req', None, 'tp'), may hold values from -12 to 12
- norm_gain: float32 [8192], replicated, may hold values from 0.5 to 4
- out_weight: bfloat16 [4096, 8192], P('tp'), may hold values from -0.09375 to 0.09375
- prev_feature: bfloat16 [64, 8192], P('req'), may hold values from -5 to 5
- draft_weight: bfloat16 [8192, 8192], P('req', 'tp'), may hold values from -0.0625 to 0.0625
- first_moment: float32 [8192, 8192], P('req', 'tp'), may hold values from -5 to 5
- second_moment: float32 [8192, 8192], P('req', 'tp'), may hold values from 0.25 to 4
Outputs:
- features: bfloat16 [64, 32, 8192], P('req', None, 'tp')
- new_weight: bfloat16 [8192, 8192], P('req', 'tp')
- new_first: float32 [8192, 8192], P('req', 'tp')
- new_second: float32 [8192, 8192], P('req', 'tp')
- draft_loss: float32 [], replicated
Inputs may be any that keep to these rules, and one draw needn't show every extreme that they name: parents[r, 0] = -1; for i of 1 or more, parents[r, i] lies in 0 to i - 1; node 31 is a child of node 30.
All inputs are finite; a program needn't handle non-finite values.
Results may differ from a plain program's by a relative error of at most 0.014.
Values may be sent and summed in bfloat16 or wider, within the bound.
No kernel may reach another device: no remote copies, remote signals or barrier semaphores. Data moves between devices by JAX's collectives and lax.ppermute only.
A program may use at most 128 MiB of HBM per device.

v0:
```python
import math
import jax
import jax.numpy as jnp
from jax import lax
from jax.sharding import PartitionSpec as P

HEADS = 32
KV_HEADS = 4
HEAD = 128
NODES = 32
CACHE = 4096
NEG_FILL = -1e30
NORM_EPSILON = 1e-06
BETA_ONE = 0.9
BETA_TWO = 0.95
CORRECT_ONE = 1.0 - 0.9**10
CORRECT_TWO = 1.0 - 0.95**10
LEARN_RATE = 0.001


def closure(parents):
    node_count = parents.shape[-1]
    onehot = (parents[:, :, None] == jnp.arange(node_count, dtype=jnp.int32)[None, None, :]).astype(
        jnp.float32
    )
    reach_map = jnp.eye(node_count, dtype=jnp.float32)[None] + onehot
    for repeat in range(node_count.bit_length()):
        reach_map = jnp.minimum(
            jnp.einsum("rij,rjk->rik", reach_map, reach_map, precision=lax.Precision.HIGHEST), 1.0
        )
    return reach_map


def body(
    queries,
    cache_keys,
    cache_values,
    tree_keys,
    tree_values,
    parents,
    lengths,
    accepted_leaf,
    residual,
    norm_gain,
    out_weight,
    prev_feature,
    draft_weight,
    first_moment,
    second_moment,
):
    full_residual = lax.all_gather(residual, "tp", axis=2, tiled=True)
    requests = queries.shape[0]
    row_count = requests * NODES
    groups = HEADS // KV_HEADS
    score_scale = 1.0 / math.sqrt(HEAD)
    tp_rank = lax.axis_index("tp")
    cache_span = cache_keys.shape[1]
    tree_span = tree_keys.shape[1]
    reach_map = closure(parents)
    query_view = queries.reshape(requests, NODES, KV_HEADS, groups, HEAD)
    cache_view = cache_keys.reshape(requests, cache_span, KV_HEADS, HEAD)
    tree_view = tree_keys.reshape(requests, tree_span, KV_HEADS, HEAD)
    cache_scores = (
        jnp.einsum("rnkgd,rckd->rkgnc", query_view, cache_view, preferred_element_type=jnp.float32)
        * score_scale
    )
    tree_scores = (
        jnp.einsum("rnkgd,rjkd->rkgnj", query_view, tree_view, preferred_element_type=jnp.float32)
        * score_scale
    )
    positions = tp_rank * cache_span + jnp.arange(cache_span, dtype=jnp.int32)
    cache_live = (positions[None, :] < lengths[:, None])[:, None, None, None, :]
    visible = lax.dynamic_slice_in_dim(reach_map, tp_rank * tree_span, tree_span, 2)
    tree_live = (visible > 0.5)[:, None, None, :, :]
    cache_scores = jnp.where(cache_live, cache_scores, NEG_FILL)
    tree_scores = jnp.where(tree_live, tree_scores, NEG_FILL)
    local_top = jnp.maximum(jnp.max(cache_scores, axis=-1), jnp.max(tree_scores, axis=-1))
    row_top = lax.pmax(local_top, "tp")
    cache_probs = jnp.where(cache_live, jnp.exp(cache_scores - row_top[..., None]), 0.0).astype(
        jnp.bfloat16
    )
    tree_probs = jnp.where(tree_live, jnp.exp(tree_scores - row_top[..., None]), 0.0).astype(
        jnp.bfloat16
    )
    totals = jnp.sum(cache_probs, axis=-1, dtype=jnp.float32) + jnp.sum(
        tree_probs, axis=-1, dtype=jnp.float32
    )
    value_view = cache_values.reshape(requests, cache_span, KV_HEADS, HEAD)
    tree_value_view = tree_values.reshape(requests, tree_span, KV_HEADS, HEAD)
    weighted = jnp.einsum(
        "rkgnc,rckd->rnkgd", cache_probs, value_view, preferred_element_type=jnp.float32
    )
    weighted = weighted + jnp.einsum(
        "rkgnj,rjkd->rnkgd", tree_probs, tree_value_view, preferred_element_type=jnp.float32
    )
    weighted = weighted.reshape(row_count, HEADS * HEAD)
    totals = jnp.transpose(totals, (0, 3, 1, 2)).reshape(row_count, HEADS)
    head_sums, head_totals = (
        lax.psum_scatter(weighted, "tp", scatter_dimension=1, tiled=True),
        lax.psum_scatter(totals, "tp", scatter_dimension=1, tiled=True),
    )
    own_heads = head_totals.shape[1]
    attended = (head_sums.reshape(row_count, own_heads, HEAD) / head_totals[:, :, None]).astype(
        jnp.bfloat16
    )
    partial_value = jnp.dot(
        attended.reshape(row_count, own_heads * HEAD),
        out_weight,
        preferred_element_type=jnp.float32,
    )
    partial_value = lax.optimization_barrier(partial_value.astype(jnp.bfloat16)).astype(jnp.float32)
    model_width = partial_value.shape[1]
    block_width = model_width // lax.axis_size("tp")
    summed = lax.psum(partial_value.astype(jnp.bfloat16), "tp").astype(jnp.float32)
    mixed = full_residual.reshape(row_count, model_width).astype(jnp.float32) + summed
    mean_sq = jnp.mean(mixed * mixed, axis=1, keepdims=True)
    features = (mixed * lax.rsqrt(mean_sq + NORM_EPSILON) * norm_gain[None, :]).astype(jnp.bfloat16)
    own_block = lax.dynamic_slice_in_dim(features, tp_rank * block_width, block_width, 1)
    feature_table = jnp.concatenate(
        [prev_feature[:, None, :], features.reshape(requests, NODES, model_width)], axis=1
    )
    inputs = jnp.take_along_axis(feature_table, (parents + 1)[:, :, None], axis=1).reshape(
        row_count, model_width
    )
    leaf_hot = (accepted_leaf[:, None] == jnp.arange(NODES, dtype=jnp.int32)[None, :]).astype(
        jnp.float32
    )
    accepted = jnp.einsum("rn,rnj->rj", leaf_hot, reach_map, precision=lax.Precision.HIGHEST)
    fill_share = 0.5 + lengths.astype(jnp.float32) / CACHE
    weights = ((1.0 + 3.0 * accepted) * fill_share[:, None]).reshape(row_count, 1)
    columns = inputs
    predicted = jnp.dot(
        columns,
        lax.all_gather(draft_weight, "req", axis=0, tiled=True),
        preferred_element_type=jnp.float32,
    )
    pred_error = predicted - own_block.astype(jnp.float32)
    scaled_err = (weights * pred_error).astype(jnp.bfloat16)
    columns = inputs
    gradient = lax.psum_scatter(
        lax.dot_general(
            columns, scaled_err, (((0,), (0,)), ((), ())), preferred_element_type=jnp.float32
        ),
        "req",
        scatter_dimension=0,
        tiled=True,
    )
    square_total, error_total = lax.psum(
        (jnp.sum(gradient * gradient), jnp.sum(weights * pred_error * pred_error)), ("req", "tp")
    )
    draft_loss = 0.5 * error_total / (row_count * lax.axis_size("req") * model_width)
    grad_norm = jnp.sqrt(square_total) + 1e-06
    clip_factor = jnp.minimum(1.0, model_width / grad_norm)
    clipped = gradient * clip_factor
    new_first = BETA_ONE * first_moment + (1.0 - BETA_ONE) * clipped
    new_second = BETA_TWO * second_moment + (1.0 - BETA_TWO) * clipped * clipped
    direction = new_first / CORRECT_ONE / (jnp.sqrt(new_second / CORRECT_TWO) + 1e-08)
    new_weight = (draft_weight.astype(jnp.float32) - LEARN_RATE * direction).astype(jnp.bfloat16)
    return (
        own_block.reshape(requests, NODES, block_width),
        new_weight,
        new_first,
        new_second,
        draft_loss,
    )


def solution(mesh):
    placed = (
        P("req", None, None),
        P("req", "tp", None),
        P("req", "tp", None),
        P("req", "tp", None),
        P("req", "tp", None),
        P("req", None),
        P("req"),
        P("req"),
        P("req", None, "tp"),
        P(),
        P("tp", None),
        P("req", None),
        P("req", "tp"),
        P("req", "tp"),
        P("req", "tp"),
    )
    return jax.shard_map(
        body,
        mesh=mesh,
        in_specs=placed,
        out_specs=(P("req", None, "tp"), P("req", "tp"), P("req", "tp"), P("req", "tp"), P()),
        check_vma=False,
    )
```

profile of v0, /device:TPU:1, one launch (start us, length us, event | category | flops | bytes accessed | tf_op | source)
XLA Modules:
  0.0 868.4 jit_solution(2874297902461404456)
XLA Ops:
  7.3 1.1 convolution_minimum_fusion.4
  8.4 0.1 copy.91
  8.5 0.3 convolution_minimum_fusion.3
  8.9 0.3 convolution_minimum_fusion.2
  9.2 0.1 copy.93
  9.3 0.3 convolution_minimum_fusion.1
  9.6 0.1 copy.94
  9.7 0.3 convolution_minimum_fusion
  10.0 0.1 copy.95
  10.1 0.2 fusion.19
  10.4 1.4 copy.89
  11.8 1.1 reshape.107
  13.0 0.3 reshape.110
  13.3 1.5 fusion.38
  14.8 4.1 bitcast_reduce_fusion
  19.0 67.8 %pmax.7 = f32[4,4,8,32]{3,2,1,0:T(8,128)S(1)} all-reduce(f32[4,4,8,32]{3,2,1,0:T(8,128)S(1)} %max.5), channel_id=1, replica_groups=mesh['req'=16,'tp'=16] {'tp'}, use_global_device_ids=true, to_apply=%region_2.3 | all-reduce | flops 4096 | bytes 32768 | tf_op jit(solution)/shard_map/pmax | solution.py:78
  86.7 0.3 convert_reduce_fusion.1
  87.0 3.0 fusion.6
  90.0 0.5 add_bitcast_fusion
  90.5 1.2 copy.74
  91.7 1.5 reshape.112
  93.3 0.7 all-gather.3.cloned.1.call-update
  94.1 3.1 convert_reduce_fusion
  97.3 0.1 reshape.113
  97.4 0.6 dynamic-slice
  98.6 61.0 %all-reduce = f32[128,32]{0,1:T(8,128)S(1)} all-reduce(f32[128,32]{0,1:T(8,128)S(1)} %reshape.113), channel_id=3, replica_groups=mesh['req'=16,'tp'=16] {'tp'}, use_global_device_ids=true, to_apply=%region_6.7.clone | all-reduce | flops 4096 | bytes 32768
  159.6 0.1 copy.76
  159.7 23.9 %reduce-scatter.3.cloned.1.call-done = f32[128,256]{1,0:T(8,128)} async-done(((f32[128,4096]{1,0:T(8,128)}), f32[128,256]{1,0:T(8,128)}) %reduce-scatter.3.cloned.1.call-update) | async-done | bytes 131088 | tf_op jit(solution)/shard_map/reduce_scatter | solution.py:99
  183.7 0.2 div.41
  183.9 4.3 convolution_convert_fusion
  188.3 0.5 all-gather.5.cloned.1.call-update
  188.8 0.2 reduce-scatter.5.cloned.1.call-start
  189.3 0.2 fusion.17
  189.7 75.2 %all-gather.3.cloned.1.call-done = bf16[4,32,8192]{2,1,0:T(8,128)(2,1)} async-done(((bf16[4,32,512]{2,1,0:T(8,128)(2,1)}), bf16[4,32,8192]{2,1,0:T(8,128)(2,1)}) %all-gather.3.cloned.1.call-update) | async-done | bytes 2097168 | tf_op jit(solution)/shard_map/all_gather | solution.py:51
  264.8 168.2 %all-reduce.4.cloned.1.call-done = bf16[128,8192]{1,0:T(8,128)(2,1)} async-done(((bf16[128,8192]{1,0:T(8,128)(2,1)}), bf16[128,8192]{1,0:T(8,128)(2,1)}) %all-reduce.4.cloned.1.call-update) | async-done | bytes 2097168 | tf_op jit(solution)/shard_map/psum | solution.py:114
  433.0 3.1 multiply_reduce_fusion
  436.2 1.0 multiply_convert_fusion
  437.2 1.6 copy.77
  438.9 1.4 pad_maximum_fusion
  440.3 8.3 gather_fusion
  448.5 0.9 constant_dynamic-slice_fusion.1
  449.5 103.7 %all-gather.5.cloned.1.call-done = bf16[8192,512]{1,0:T(8,128)(2,1)} async-done(((bf16[512,512]{1,0:T(8,128)(2,1)}), bf16[8192,512]{1,0:T(8,128)(2,1)}) %all-gather.5.cloned.1.call-update) | async-done | bytes 8388624 | tf_op jit(solution)/shard_map/all_gather | solution.py:134
  553.2 6.2 fusion.13
  559.4 8.2 fusion.12
  567.6 210.0 %reduce-scatter.5.cloned.1.call-done = f32[512,512]{1,0:T(8,128)} async-done(((f32[8192,512]{1,0:T(8,128)}), f32[512,512]{1,0:T(8,128)}) %reduce-scatter.5.cloned.1.call-update) | async-done | bytes 1048592 | tf_op jit(solution)/shard_map/reduce_scatter | solution.py:140
  777.6 2.1 multiply_reduce_fusion.1
  779.7 76.2 %all-reduce.1 = (f32[]{:T(128)}, f32[]{:T(128)}) all-reduce(f32[]{:T(128)} %multiply_reduce_fusion.1, f32[]{:T(128)} %get-tuple-element.16), channel_id=1, replica_groups=mesh['req'=16,'tp'=16] {'req','tp'}, use_global_device_ids=true, to_apply=%region_11.12 | all-reduce | flops 2 | bytes 16 | tf_op jit(solution)/shard_map/psum | solution.py:148
  857.3 3.4 subtract_convert_fusion
  (65 shorter events, 1.1 us)
Async XLA Ops:
  7.2 82.8 %copy-start = (bf16[4,2,512]{2,1,0:T(2,128)(2,1)S(1)}, bf16[4,2,512]{2,1,0:T(2,128)(2,1)}, u32[]{:S(2)}) copy-start(bf16[4,2,512]{2,1,0:T(2,128)(2,1)} %param.19) | copy-start | bytes 24580
  7.2 4.7 copy-start.9
  7.2 5.8 copy-start.10
  7.2 6.0 copy-start.15
  7.2 6.1 copy-start.16
  7.2 176.4 %reduce-scatter.3.cloned.1.call-start = ((), (), s32[]{:S(2)}) async-start(), calls=%async_computation.3 | async-start | bytes 2228224 | tf_op jit(solution)/shard_map/reduce_scatter | solution.py:99
  93.2 4.2 copy-start.18
  93.3 171.5 %all-gather.3.cloned.1.call-start = ((), (), s32[]{:S(2)}) async-start(), calls=%async_computation.2 | async-start | bytes 2228224 | tf_op jit(solution)/shard_map/all_gather | solution.py:51
  94.0 338.9 %all-reduce.4.cloned.1.call-start = ((), (), s32[]{:S(2)}) async-start(), calls=%async_computation.4 | async-start | bytes 4194304 | tf_op jit(solution)/shard_map/psum | solution.py:114
  183.9 5.2 copy-start.14
  183.9 5.4 copy-start.17
  188.2 247.9 %copy-start.13 = (f32[8192]{0:T(1024)S(1)}, f32[8192]{0:T(1024)}, u32[]{:S(2)}) copy-start(f32[8192]{0:T(1024)} %param.24) | copy-start | bytes 98308
  188.2 365.0 %all-gather.5.cloned.1.call-start = ((), (), s32[]{:S(2)}) async-start(), calls=%async_computation.5 | async-start | bytes 8912896 | tf_op jit(solution)/shard_map/all_gather | solution.py:134
  188.8 588.8 %reduce-scatter.5.cloned.1.call-start = ((), (), s32[]{:S(2)}) async-start(), calls=%async_computation.6 | async-start | bytes 17825792 | tf_op jit(solution)/shard_map/reduce_scatter | solution.py:140
  264.8 171.3 %copy-start.4 = (bf16[4,32,8192]{2,1,0:T(8,128)(2,1)S(1)}, bf16[4,32,8192]{2,1,0:T(8,128)(2,1)}, u32[]{:S(2)}) copy-start(bf16[4,32,8192]{2,1,0:T(8,128)(2,1)} %all-gather.3.cloned.1.call-done) | copy-start | bytes 6291460
  433.0 3.2 copy-start.5
  436.1 2.7 copy-start.12
  437.2 1.6 copy-start.3
  449.5 109.9 %copy-start.11 = (bf16[128,512]{1,0:T(8,128)(2,1)}, bf16[128,512]{1,0:T(8,128)(2,1)S(1)}, u32[]{:S(2)}) copy-start(bf16[128,512]{1,0:T(8,128)(2,1)S(1)} %constant_dynamic-slice_fusion.1) | copy-start | bytes 393220
  449.5 109.9 %copy-start.2 = (bf16[128,8192]{1,0:T(8,128)(2,1)S(1)}, bf16[128,8192]{1,0:T(8,128)(2,1)}, u32[]{:S(2)}) copy-start(bf16[128,8192]{1,0:T(8,128)(2,1)} %gather_fusion) | copy-start | bytes 6291460
  567.6 289.7 %copy-start.6 = (bf16[512,512]{1,0:T(8,128)(2,1)S(1)}, bf16[512,512]{1,0:T(8,128)(2,1)}, u32[]{:S(2)}) copy-start(bf16[512,512]{1,0:T(8,128)(2,1)} %param.27) | copy-start | bytes 1572868
  567.6 289.7 %copy-start.7 = (f32[512,512]{1,0:T(8,128)S(1)}, f32[512,512]{1,0:T(8,128)}, u32[]{:S(2)}) copy-start(f32[512,512]{1,0:T(8,128)} %param.28) | copy-start | bytes 3145732
  567.6 289.7 %copy-start.8 = (f32[512,512]{1,0:T(8,128)S(1)}, f32[512,512]{1,0:T(8,128)}, u32[]{:S(2)}) copy-start(f32[512,512]{1,0:T(8,128)} %param.29) | copy-start | bytes 3145732
  567.6 293.1 %copy-start.1 = (bf16[4,2,512]{2,1,0:T(2,128)(2,1)S(1)}, bf16[4,2,512]{2,1,0:T(2,128)(2,1)}, u32[]{:S(2)}) copy-start(bf16[4,2,512]{2,1,0:T(2,128)(2,1)} %param.19) | copy-start | bytes 24580
Sparse Core Ops, SparseCore 0:
  93.4 90.2 reduce-scatter.2
  185.5 79.3 all-gather.2
  267.5 165.4 all-reduce.3
  435.6 117.5 all-gather.4
  567.7 209.8 reduce-scatter.4
where the time goes:
time: 869 us; the launch traced here: 868 us
  waiting for transfers between devices  582 us (67%)
  blocking collectives  205 us (24%)
  matrix products  30.4 us (3%)
  local copies, waits for them, and re-layouts  18.2 us (2%)
  between operations  17.4 us (2%)
  other arithmetic  14.8 us (2%)
    reduce_scatter x1, waiting for transfers between devices, body(): lax.psum_scatter(lax.dot_general(columns, scaled_err, (((0,), (0,)), ((),...  210 us
    psum x1, waiting for transfers between devices, body(): lax.psum(partial_value.astype(jnp.bfloat16), 'tp').astype(jnp.float32)  168 us
    all_gather x1, waiting for transfers between devices, body(): lax.all_gather(draft_weight, 'req', axis=0, tiled=True)  104 us
    psum x1, blocking collectives, body(): lax.psum((jnp.sum(gradient * gradient), jnp.sum(weights * pred_error * pr...  76.2 us
    all_gather x1, waiting for transfers between devices, body(): full_residual = lax.all_gather(residual, 'tp', axis=2, tiled=True)  75.2 us
    pmax x1, blocking collectives, body(): row_top = lax.pmax(local_top, 'tp')  67.8 us
    unnamed x1, blocking collectives  61 us
    reduce_scatter x1, waiting for transfers between devices, body(): lax.psum_scatter(weighted, 'tp', scatter_dimension=1, tiled=True)  23.9 us
  transfers between devices with their start and end apart: 5, of which 5 were waited for; matrix products, arithmetic and copies ran while one was open for 3% of the time, Pallas kernels for 0%

commit v1 on v0

--- a/solution.py
+++ b/solution.py
@@ -111,7 +111,9 @@
     partial_value = lax.optimization_barrier(partial_value.astype(jnp.bfloat16)).astype(jnp.float32)
     model_width = partial_value.shape[1]
     block_width = model_width // lax.axis_size("tp")
-    summed = lax.psum(partial_value.astype(jnp.bfloat16), "tp").astype(jnp.float32)
+    summed = jnp.sum(lax.all_gather(partial_value.astype(jnp.bfloat16), "tp"), axis=0).astype(
+        jnp.float32
+    )
     mixed = full_residual.reshape(row_count, model_width).astype(jnp.float32) + summed
     mean_sq = jnp.mean(mixed * mixed, axis=1, keepdims=True)
     features = (mixed * lax.rsqrt(mean_sq + NORM_EPSILON) * norm_gain[None, :]).astype(jnp.bfloat16)

time: 869 us -> 1050 us (1.21)
  waiting for transfers between devices: 582 us -> 734 us
  other arithmetic: 14.8 us -> 36.2 us
    all_gather x0 -> x1, waiting for transfers between devices: none -> 362 us  [body(): lax.all_gather(partial_value.astype(jnp.bfloat16), 'tp')]
    psum x1 -> x0, waiting for transfers between devices: 168 us -> none  [body(): lax.psum(partial_value.astype(jnp.bfloat16), 'tp').astype(jnp.float32)]
    all_gather x1, waiting for transfers between devices: 104 us -> 71 us  [body(): lax.all_gather(draft_weight, 'req', axis=0, tiled=True)]
    reduce_sum x0 -> x1, other arithmetic: none -> 12.9 us  [body(): jnp.sum(lax.all_gather(partial_value.astype(jnp.bfloat16), 'tp'), axis=0)]
  transfers between devices with their start and end apart: 5 -> 5, of which waited for: 5 -> 5; matrix products, arithmetic and copies ran while one was open for 3% -> 5% of each run, Pallas kernels for 0% -> 0%
where the time goes in v1:
time: 1050 us; the launch traced here: 1040 us
  waiting for transfers between devices  734 us (70%)
  blocking collectives  205 us (20%)
  other arithmetic  36.2 us (3%)
  matrix products  28.9 us (3%)
  local copies, waits for them, and re-layouts  22.5 us (2%)
  between operations  17.4 us (2%)
    all_gather x1, waiting for transfers between devices, body(): lax.all_gather(partial_value.astype(jnp.bfloat16), 'tp')  362 us
    reduce_scatter x1, waiting for transfers between devices, body(): lax.psum_scatter(lax.dot_general(columns, scaled_err, (((0,), (0,)), ((),...  210 us
    psum x1, blocking collectives, body(): lax.psum((jnp.sum(gradient * gradient), jnp.sum(weights * pred_error * pr...  76.2 us
    all_gather x1, waiting for transfers between devices, body(): lax.all_gather(draft_weight, 'req', axis=0, tiled=True)  71 us
    pmax x1, blocking collectives, body(): row_top = lax.pmax(local_top, 'tp')  67.8 us
    all_gather x1, waiting for transfers between devices, body(): full_residual = lax.all_gather(residual, 'tp', axis=2, tiled=True)  66.7 us
    unnamed x1, blocking collectives  60.9 us
    reduce_scatter x1, waiting for transfers between devices, body(): lax.psum_scatter(weighted, 'tp', scatter_dimension=1, tiled=True)  24.2 us
  transfers between devices with their start and end apart: 5, of which 5 were waited for; matrix products, arithmetic and copies ran while one was open for 5% of the time, Pallas kernels for 0%

profile of v1, /device:TPU:1, one launch (start us, length us, event | category | flops | bytes accessed | tf_op | source)
XLA Modules:
  0.0 1044.6 jit_solution(10009738151687288507)
XLA Ops:
  7.3 1.1 convolution_minimum_fusion.4
  8.3 0.1 copy.104
  8.4 0.3 convolution_minimum_fusion.3
  8.8 0.3 convolution_minimum_fusion.2
  9.2 0.3 convolution_minimum_fusion.1
  9.6 0.3 convolution_minimum_fusion
  10.0 0.2 fusion.22
  10.3 1.4 copy.102
  11.8 0.3 reshape.127
  12.2 1.5 fusion.41
  13.7 2.9 bitcast_reduce_fusion
  16.6 67.8 %pmax.7 = f32[4,4,8,32]{3,2,1,0:T(8,128)S(1)} all-reduce(f32[4,4,8,32]{3,2,1,0:T(8,128)S(1)} %max.5), channel_id=1, replica_groups=mesh['req'=16,'tp'=16] {'tp'}, use_global_device_ids=true, to_apply=%region_2.3 | all-reduce | flops 4096 | bytes 32768 | tf_op jit(solution)/shard_map/pmax | solution.py:78
  84.3 0.3 reshape.130
  84.6 0.3 convert_reduce_fusion.1
  84.9 2.9 fusion.6
  87.9 0.5 add_bitcast_fusion
  88.4 1.2 copy.85
  89.6 1.5 reshape.132
  91.2 0.8 copy.60
  92.1 3.1 convert_reduce_fusion
  95.3 0.1 reshape.133
  95.4 0.6 dynamic-slice
  96.6 60.9 %all-reduce = f32[128,32]{0,1:T(8,128)S(1)} all-reduce(f32[128,32]{0,1:T(8,128)S(1)} %reshape.133), channel_id=4, replica_groups=mesh['req'=16,'tp'=16] {'tp'}, use_global_device_ids=true, to_apply=%region_6.7.clone | all-reduce | flops 4096 | bytes 32768
  157.6 0.1 copy.87
  157.7 24.2 %reduce-scatter.3.cloned.1.call-done = f32[128,256]{1,0:T(8,128)} async-done(((f32[128,4096]{1,0:T(8,128)}), f32[128,256]{1,0:T(8,128)}) %reduce-scatter.3.cloned.1.call-update) | async-done | bytes 131088 | tf_op jit(solution)/shard_map/reduce_scatter | solution.py:99
  181.9 0.2 div.41
  182.1 4.3 convolution_convert_fusion
  186.5 0.5 all-gather.7.cloned.1.call-update
  187.0 0.2 reduce-scatter.5.cloned.1.call-start
  187.4 0.2 fusion.20
  187.9 66.7 %all-gather.5.cloned.1.call-done = bf16[4,32,8192]{2,0,1:T(4,128)(2,1)} async-done(((bf16[4,32,512]{2,0,1:T(4,128)(2,1)}), bf16[4,32,8192]{2,0,1:T(4,128)(2,1)}) %all-gather.5.cloned.1.call-update) | async-done | bytes 2097168 | tf_op jit(solution)/shard_map/all_gather | solution.py:51
  254.7 4.7 copy.61
  259.4 361.9 %all-gather.9.cloned.1.call-done = bf16[2048,8192]{1,0:T(8,128)(2,1)} async-done(((bf16[128,8192]{1,0:T(8,128)(2,1)}), bf16[2048,8192]{1,0:T(8,128)(2,1)}) %all-gather.9.cloned.1.call-update) | async-done | bytes 33554448 | tf_op jit(solution)/shard_map/all_gather | solution.py:114
  621.3 12.9 %reduce_sum.59 = bf16[128,8192]{1,0:T(8,128)(2,1)} reduce(bf16[16,128,8192]{2,1,0:T(8,128)(2,1)} %bitcast.71, bf16[]{:T(256)} %constant.16.clone.1), dimensions={0}, to_apply=%region_7.8 | reduce | flops 15728640 | bytes 35651584 | tf_op jit(solution)/shard_map/reduce_sum | solution.py:114
  634.3 2.3 convert_element_type.85
  636.5 1.9 copy-done.2
  638.5 2.9 multiply_reduce_fusion
  641.6 6.3 multiply_convert_fusion
  647.9 1.4 pad_maximum_fusion
  649.3 8.2 gather_fusion
  657.5 1.1 fusion.16
  658.6 71.0 %all-gather.7.cloned.1.call-done = bf16[8192,512]{1,0:T(8,128)(2,1)} async-done(((bf16[512,512]{1,0:T(8,128)(2,1)}), bf16[8192,512]{1,0:T(8,128)(2,1)}) %all-gather.7.cloned.1.call-update) | async-done | bytes 8388624 | tf_op jit(solution)/shard_map/all_gather | solution.py:136
  729.6 6.0 fusion.13
  735.6 8.2 fusion.12
  743.8 210.0 %reduce-scatter.5.cloned.1.call-done = f32[512,512]{1,0:T(8,128)} async-done(((f32[8192,512]{1,0:T(8,128)}), f32[512,512]{1,0:T(8,128)}) %reduce-scatter.5.cloned.1.call-update) | async-done | bytes 1048592 | tf_op jit(solution)/shard_map/reduce_scatter | solution.py:142
  953.8 2.1 multiply_reduce_fusion.1
  955.9 76.2 %all-reduce.1 = (f32[]{:T(128)}, f32[]{:T(128)}) all-reduce(f32[]{:T(128)} %multiply_reduce_fusion.1, f32[]{:T(128)} %get-tuple-element.16), channel_id=1, replica_groups=mesh['req'=16,'tp'=16] {'req','tp'}, use_global_device_ids=true, to_apply=%region_11.12 | all-reduce | flops 2 | bytes 16 | tf_op jit(solution)/shard_map/psum | solution.py:150
  1033.5 3.4 subtract_convert_fusion
  (71 shorter events, 1.6 us)
Async XLA Ops:
  7.2 80.7 %copy-start = (bf16[4,2,512]{2,1,0:T(2,128)(2,1)S(1)}, bf16[4,2,512]{2,1,0:T(2,128)(2,1)}, u32[]{:S(2)}) copy-start(bf16[4,2,512]{2,1,0:T(2,128)(2,1)} %param.19) | copy-start | bytes 24580
  7.2 4.6 copy-start.8
  7.2 4.9 copy-start.15
  7.2 5.0 copy-start.16
  7.2 174.6 %reduce-scatter.3.cloned.1.call-start = ((), (), s32[]{:S(2)}) async-start(), calls=%async_computation.3 | async-start | bytes 2228224 | tf_op jit(solution)/shard_map/reduce_scatter | solution.py:99
  12.2 72.2 %copy-start.9 = (bf16[4,256,512]{2,1,0:T(8,128)(2,1)S(1)}, bf16[4,256,512]{2,1,0:T(8,128)(2,1)}, u32[]{:S(2)}) copy-start(bf16[4,256,512]{2,1,0:T(8,128)(2,1)} %param.17) | copy-start | bytes 3145732
  89.6 1.6 copy-start.11
  91.1 4.2 copy-start.18
  91.2 163.5 %all-gather.5.cloned.1.call-start = ((), (), s32[]{:S(2)}) async-start(), calls=%async_computation.2 | async-start | bytes 2228224 | tf_op jit(solution)/shard_map/all_gather | solution.py:51
  92.0 529.3 %all-gather.9.cloned.1.call-start = ((), (), s32[]{:S(2)}) async-start(), calls=%async_computation.6 | async-start | bytes 35651584 | tf_op jit(solution)/shard_map/all_gather | solution.py:114
  182.1 5.2 copy-start.14
  182.1 5.3 copy-start.17
  182.1 5.8 copy-start.13
  186.4 543.2 %all-gather.7.cloned.1.call-start = ((), (), s32[]{:S(2)}) async-start(), calls=%async_computation.4 | async-start | bytes 8912896 | tf_op jit(solution)/shard_map/all_gather | solution.py:136
  187.0 766.8 %reduce-scatter.5.cloned.1.call-start = ((), (), s32[]{:S(2)}) async-start(), calls=%async_computation.5 | async-start | bytes 17825792 | tf_op jit(solution)/shard_map/reduce_scatter | solution.py:142
  634.3 4.2 copy-start.3
  636.5 1.9 copy-start.2
  641.6 6.3 copy-start.12
  658.6 77.0 %copy-start.10 = (bf16[128,512]{1,0:T(8,128)(2,1)}, bf16[128,512]{1,0:T(8,128)(2,1)S(1)}, u32[]{:S(2)}) copy-start(bf16[128,512]{1,0:T(8,128)(2,1)S(1)} %fusion.16) | copy-start | bytes 393220
  658.6 77.0 %copy-start.4 = (bf16[128,8192]{1,0:T(8,128)(2,1)S(1)}, bf16[128,8192]{1,0:T(8,128)(2,1)}, u32[]{:S(2)}) copy-start(bf16[128,8192]{1,0:T(8,128)(2,1)} %gather_fusion) | copy-start | bytes 6291460
  743.8 289.7 %copy-start.5 = (bf16[512,512]{1,0:T(8,128)(2,1)S(1)}, bf16[512,512]{1,0:T(8,128)(2,1)}, u32[]{:S(2)}) copy-start(bf16[512,512]{1,0:T(8,128)(2,1)} %param.27) | copy-start | bytes 1572868
  743.8 289.8 %copy-start.6 = (f32[512,512]{1,0:T(8,128)S(1)}, f32[512,512]{1,0:T(8,128)}, u32[]{:S(2)}) copy-start(f32[512,512]{1,0:T(8,128)} %param.28) | copy-start | bytes 3145732
  743.8 289.8 %copy-start.7 = (f32[512,512]{1,0:T(8,128)S(1)}, f32[512,512]{1,0:T(8,128)}, u32[]{:S(2)}) copy-start(f32[512,512]{1,0:T(8,128)} %param.29) | copy-start | bytes 3145732
  743.8 293.1 %copy-start.1 = (bf16[4,2,512]{2,1,0:T(2,128)(2,1)S(1)}, bf16[4,2,512]{2,1,0:T(2,128)(2,1)}, u32[]{:S(2)}) copy-start(bf16[4,2,512]{2,1,0:T(2,128)(2,1)} %param.19) | copy-start | bytes 24580
Sparse Core Ops, SparseCore 0:
  91.3 90.5 reduce-scatter.2
  184.2 70.4 all-gather.4
  256.4 364.8 all-gather.8
  623.9 105.6 all-gather.6
  743.9 209.8 reduce-scatter.4
